TPU v7x, 32 devices: a whole 2x2x4 slice. The times are simulated.
32 devices in a mesh: groups: 2 (over x), row: 8 (over z, y), col: 2 (over core).
Axes of the slice: x: 2, y: 2, z: 4, core: 2. Of those that a mesh axis runs over, the one named last changes fastest.
Arguments:
- queries: bfloat16 [4096, 2560], P(('groups', 'row', 'col')), parts along dimension 0, may hold values from -32 to 32
- keys: bfloat16 [4096, 2560], P(('groups', 'row', 'col')), parts along dimension 0, may hold values from -6 to 6
- values: bfloat16 [4096, 2560], P(('groups', 'row', 'col')), parts along dimension 0, may hold values from -6 to 6
- pattern: int32 [16, 5], P('groups'), parts along dimension 0, may hold values from 0 to 1, as said below
Outputs:
- attended: bfloat16 [4096, 2560], P(('groups', 'row', 'col')), parts along dimension 0
There are 2 independent parts, one for each index of `groups`. A program takes and returns all parts, laid end to end along the dimension named above; each array names one. Nothing has to cross between parts.
Inputs may be any that keep to these rules, and one draw needn't show every extreme that they name: pattern[r, 0] is 1; pattern[r, j] is 0 where r + off_j lies outside 0 .. 7, or where off_j is -1 or +1 and r + off_j lies in another band of 4 tile rows.
All inputs are finite; a program needn't handle non-finite values.
Results may differ from a plain program's by a relative error of at most 0.0045.
Values may be sent and summed in bfloat16 or wider, within the bound.
No kernel may reach another device: no remote copies, remote signals or barrier semaphores. Data moves between devices by JAX's collectives and lax.ppermute only.
A program may use at most 64 MiB of HBM per device.

v0:
```python
import functools

import jax
import jax.numpy as jnp
from jax import lax
from jax.experimental import pallas as pl
from jax.experimental.pallas import tpu as pltpu
from jax.sharding import PartitionSpec as P


HD = 128
TILE_H = 4
OFFSETS = (0, -1, 1, -TILE_H, TILE_H)
SCALE = HD ** (-0.5) * 1.4426950408889634
FAR_BELOW = -1e30
HEADS_AT_ONCE = 4
PARTS = 2
VMEM_BYTES = 16 * 1024 * 1024


def plan(rows):
    near, back, cross, far = {}, {}, {}, [({}, {}), ({}, {})]
    visit, side = {}, {}
    for row in range(rows):
        other, start = row ^ 1, row - row % TILE_H
        if row % TILE_H in (1, 2):
            back[other] = row
            visit[row] = OFFSETS.index(other - row)
            other = 2 * start + TILE_H - 1 - row
            if other < rows:
                cross[other] = row
                side[row] = OFFSETS.index(other - row)
        elif other < rows:
            near[other] = row
            side[row] = OFFSETS.index(other - row)
        for way in (0, 1):
            other = row + TILE_H if (row // TILE_H) % 2 == way else row - TILE_H
            if 0 <= other < rows:
                far[way][0][other] = row
                far[way][1][row] = OFFSETS.index(other - row)
    return near, back, cross, [way for way in far if way[0]], visit, side


def lanes(value):
    return [value[:, at : at + HD] for at in range(0, value.shape[1], HD)]


def over_row(reduce, join, slices):
    found = reduce(functools.reduce(join, slices), axis=1, keepdims=True)
    return jnp.broadcast_to(found, slices[0].shape)


def gathered(pair, here):
    return jnp.concatenate(
        [functools.reduce(jnp.add, [ref[:, here] for ref in half]) for half in pair], axis=0
    )


def grouped(refs, pairs):
    refs = list(refs)
    return [[[refs.pop(0) for _ in half] for half in pair] for pair in pairs], refs


def flat(pairs):
    return [a for pair in pairs for half in pair for a in half]


def lane_of(stat_ref, lane):
    stats = stat_ref[...]
    at = lax.broadcasted_iota(jnp.int32, stats.shape, 1)
    found = jnp.sum(jnp.where(at == lane, stats, 0.0), axis=1, keepdims=True)
    return jnp.broadcast_to(found, stats.shape)


def attend_chunk(index, heads, k_pairs, visited, bias_ref, refs, score_ref, weight_ref):
    q_ref, *refs = refs
    k_refs, refs = grouped(refs, k_pairs)
    v_refs, refs = refs[:2], refs[2:]
    if visited:
        visit_ref, stat_ref, *refs = refs
    out_ref, *held_refs = refs
    keys_each = 2 * v_refs[0].shape[0]
    each = keys_each // HD
    kept = {}

    def score(head, here):
        for n, pair in enumerate(k_refs):
            found = lax.dot_general(
                q_ref[:, here],
                gathered(pair, here),
                (((1,), (1,)), ((), ())),
                preferred_element_type=jnp.float32,
            )
            found = found * SCALE
            if n > 0:
                found = found + bias_ref[n]
            score_ref[head, :, n * keys_each : (n + 1) * keys_each] = found

    def weigh(head, here):
        slices = lanes(score_ref[head])
        top = over_row(jnp.max, jnp.maximum, slices)
        if visited:
            before = lane_of(stat_ref, index * heads + head) + bias_ref[0]
            top = jnp.maximum(top, before)
        weights = [jnp.exp2(s - top) for s in slices]
        total = over_row(jnp.sum, jnp.add, weights)
        factor = None
        if visited:
            factor = jnp.exp2(before - top)
            total = total + factor
        inverse = 1.0 / total
        for at, w in enumerate(weights):
            n = at // each
            if n == 0:
                weight_ref[head, :, at * HD : (at + 1) * HD] = w.astype(jnp.bfloat16)
            else:
                start = head * keys_each + at % each * HD
                held_refs[n - 1][:, start : start + HD] = (w * inverse).astype(jnp.bfloat16)
        if not visited:
            at = lax.broadcasted_iota(jnp.int32, top.shape, 1)
            stats = held_refs[0]
            kept_stats = stats[...] if head > 0 else jnp.where(index == 0, 0.0, stats[...])
            stats[...] = jnp.where(at == index * heads + head, top + jnp.log2(total), kept_stats)
        kept[head] = (inverse, factor)

    def mix(head, here):
        inverse, factor = kept.pop(head)
        out = jnp.dot(
            weight_ref[head],
            jnp.concatenate([v[:, here] for v in v_refs], axis=0),
            preferred_element_type=jnp.float32,
        )
        if visited:
            out = out + factor * visit_ref[:, here].astype(jnp.float32)
        out_ref[:, here] = (out * inverse).astype(out_ref.dtype)

    steps = [score, weigh, mix]
    for time in range(heads + len(steps) - 1):
        for number, step in enumerate(steps):
            head = time - number
            if 0 <= head < heads:
                step(head, slice(head * HD, (head + 1) * HD))


def divisor(heads, most):
    return max(n for n in range(1, most + 1) if heads % n == 0)


def call(chunk, at_once, scalars, operands, out_types, scratch, dots, keys):
    tokens, width = operands[0].shape
    heads = divisor(width // HD, at_once)
    steps = width // (heads * HD)
    arrays = len(operands) + len(out_types)

    def kernel(*refs):
        scalar_refs, refs = refs[: len(scalars)], refs[len(scalars) :]
        array_refs, scratch_refs = refs[:arrays], refs[arrays:]

        def step(i, carry):
            views = []
            for ref in array_refs:
                wide = ref.shape[1] // steps
                whole = ref.shape[1] == HD
                at = pl.ds(pl.multiple_of(i * wide, wide), wide)
                views.append(ref if whole else ref.at[:, at])
            chunk(i, heads, scalar_refs, views, scratch_refs)
            return carry

        lax.fori_loop(0, steps, step, 0)

    whole = pl.BlockSpec(memory_space=pltpu.VMEM)
    run = pl.pallas_call(
        kernel,
        in_specs=[pl.BlockSpec(memory_space=pltpu.SMEM)] * len(scalars) + [whole] * len(operands),
        out_specs=[whole] * len(out_types),
        out_shape=out_types,
        scratch_shapes=[pltpu.VMEM((heads,) + shape, t) for shape, t in scratch],
        cost_estimate=cost(tokens, keys, width, dots),
        compiler_params=pltpu.CompilerParams(vmem_limit_bytes=VMEM_BYTES),
    )
    return list(run(*scalars, *operands))


def cost(tokens, keys, width, dots):
    return pl.CostEstimate(
        flops=dots * 2 * tokens * keys * width,
        transcendentals=tokens * keys * (width // HD),
        bytes_accessed=2 * width * (2 * tokens + dots * keys),
    )


def attend(bias, queries, k_pairs, v_own, visit):
    tokens, width = queries.shape
    held, visited = len(k_pairs) - 1, visit is not None
    keys = 2 * tokens * len(k_pairs)

    def chunk(index, heads, scalar_refs, views, scratch_refs):
        bias_ref = scalar_refs[0] if visited else None
        attend_chunk(index, heads, k_pairs, visited, bias_ref, views, *scratch_refs)

    full = jax.ShapeDtypeStruct((tokens, width), jnp.float32 if visited else jnp.bfloat16)
    weight = jax.ShapeDtypeStruct((tokens, 2 * tokens * (width // HD)), jnp.bfloat16)
    outs = [full] + [weight] * held
    outs += [] if visited else [jax.ShapeDtypeStruct((tokens, HD), jnp.float32)]
    operands = [queries] + flat(k_pairs) + flat([v_own]) + (list(visit) if visited else [])
    scratch = [((tokens, keys), jnp.float32), ((tokens, 2 * tokens), jnp.bfloat16)]
    scalars = [bias] if visited else []
    return call(chunk, HEADS_AT_ONCE, scalars, operands, outs, scratch, 2, keys)


def mix(base, weights, v_pair):
    tokens = base.shape[0]

    def chunk(index, heads, scalar_refs, views, scratch_refs):
        base_ref, weight_ref, *v_refs, out_ref = views
        pair = grouped(v_refs, [v_pair])[0][0]
        for head in range(heads):
            here = slice(head * HD, (head + 1) * HD)
            out_ref[:, here] = base_ref[:, here] + jnp.dot(
                weight_ref[:, head * 2 * tokens : (head + 1) * 2 * tokens],
                gathered(pair, here),
                preferred_element_type=jnp.float32,
            )

    outs = [jax.ShapeDtypeStruct(base.shape, base.dtype)]
    operands = [base, weights] + flat([v_pair])
    return call(chunk, 10, [], operands, outs, [], 1, 2 * tokens)[0]


def finish(part, parts, base, weights, v_pairs, dtype, so_far):
    tokens, width = base.shape
    blocks, heads = len(v_pairs), width // HD // parts
    at_once = divisor(heads, 5)
    started, cols = part * heads * HD, heads * HD

    def kernel(base_ref, *refs):
        weight_refs, refs = refs[:blocks], refs[blocks:]
        v_refs, refs = refs[: 2 * blocks], refs[2 * blocks :]
        out_ref, held_ref, sems = refs[-3:]
        keys_each = 2 * tokens
        copies = []
        for step in range(heads // at_once):
            for head in range(step * at_once, (step + 1) * at_once):
                here = slice(head * HD, (head + 1) * HD)
                there = slice(started + head * HD, started + (head + 1) * HD)
                first = (part * heads + head) * keys_each
                chosen = [v[:, here] for v in v_refs]
                out = jnp.dot(
                    jnp.concatenate([w[:, first : first + keys_each] for w in weight_refs], axis=1),
                    jnp.concatenate(chosen, axis=0),
                    preferred_element_type=jnp.float32,
                )
                held_ref[:, here] = (base_ref[:, there] + out).astype(held_ref.dtype)
            wide = at_once * HD
            copies.append(
                pltpu.make_async_copy(
                    held_ref.at[:, pl.ds(step * wide, wide)],
                    out_ref.at[:, pl.ds(started + step * wide, wide)],
                    sems.at[step],
                )
            )
            copies[-1].start()
        for copy in copies:
            copy.wait()

    whole, anywhere = pl.BlockSpec(memory_space=pltpu.VMEM), pl.BlockSpec(memory_space=pl.ANY)
    operands = [base] + weights + flat(v_pairs)
    aliases = {} if so_far is None else {len(operands): 0}
    return pl.pallas_call(
        kernel,
        in_specs=[whole] * len(operands) + [anywhere] * len(aliases),
        out_specs=anywhere,
        out_shape=jax.ShapeDtypeStruct((tokens, width), dtype),
        scratch_shapes=[
            pltpu.VMEM((tokens, cols), dtype),
            pltpu.SemaphoreType.DMA((heads // at_once,)),
        ],
        input_output_aliases=aliases,
        cost_estimate=cost(tokens, 2 * tokens * blocks, cols, 1),
        compiler_params=pltpu.CompilerParams(vmem_limit_bytes=VMEM_BYTES),
    )(*operands, *([] if so_far is None else [so_far]))


def shards(routes, queries, keys, values, pattern):
    rows = lax.axis_size("row")
    cols = lax.axis_size("col")
    row = lax.axis_index("row")
    near, back, cross, far, visit, side = routes

    def moved(value, sends):
        return lax.ppermute(value, "row", sorted(sends.items()))

    def swapped(value, sends):
        reached = range(rows) if sends is None else sorted(sends.values())
        pairs = [(r * cols + c, r * cols + cols - 1 - c) for r in reached for c in range(cols)]
        return lax.ppermute(value, ("row", "col"), pairs)

    def paired(value, sends):
        return (value,), (swapped(value, sends),)

    def joined(of_near, of_cross):
        first = paired(of_near, near)
        second = paired(of_cross, cross)
        return tuple(a + b for a, b in zip(first, second))

    own_row = lax.dynamic_index_in_dim(pattern, row, 0, keepdims=True)

    def biases(*candidates):
        table = [[given.get(r, len(OFFSETS)) for given in candidates] for r in range(rows)]
        picks = jnp.asarray(table, jnp.int32)[row]
        here = jnp.arange(len(OFFSETS), dtype=jnp.int32)[None, :] == picks[:, None]
        live = jnp.sum(jnp.where(here, own_row, 0), axis=1)
        return jnp.where(live == 1, 0.0, FAR_BELOW).astype(jnp.float32)

    cut = values.shape[1] // PARTS
    visitors = moved(queries, near)
    k_far = [moved(keys, way[0]) for way in far]
    k_cross = moved(keys, cross)
    k_near = moved(keys, near)
    v_cross = moved(values, cross)
    v_near = moved(values, near)
    k_own, v_own = paired(keys, None), paired(values, None)

    result, stats = attend(None, visitors, [k_own], v_own, None)
    visited = (moved(result, back), moved(stats, back))

    k_pairs = [k_own, joined(k_near, k_cross)]
    k_pairs += [paired(k, way[0]) for k, way in zip(k_far, far)]
    bias = biases(visit, side, *[way[1] for way in far])
    base, of_side, *weights = attend(bias, queries, k_pairs, v_own, visited)
    base = mix(base, of_side, joined(v_near, v_cross))
    out = None
    for part in range(PARTS):
        here = values[:, part * cut : (part + 1) * cut]
        v_pairs = []
        for way in far:
            v = moved(here, way[0])
            v_pairs.append(paired(v, way[0]))
        out = finish(part, PARTS, base, weights, v_pairs, queries.dtype, out)
    return out


def solution(mesh):
    placed = P(("groups", "row", "col"), None)
    routes = plan(mesh.shape["row"])

    def body(*args):
        return shards(routes, *args)

    return jax.shard_map(
        body,
        mesh=mesh,
        in_specs=(placed, placed, placed, P("groups", None)),
        out_specs=placed,
        check_vma=False,
    )
```

profile of v0, /device:TPU:0, one launch (start us, length us, event | category | flops | bytes accessed | tf_op | source)
XLA Modules:
  0.0 110.7 jit_solution(13919455166864814498)
XLA Ops:
  0.0 1.2 %fusion = (bf16[128,1280]{1,0:T(8,128)(2,1)S(1)}, bf16[128,1280]{1,0:T(8,128)(2,1)S(1)}) fusion(bf16[128,2560]{1,0:T(8,128)(2,1)} %refs_10_.1), kind=kLoop, calls=%fused_computation.5 | loop fusion | bytes 1310720 | tf_op jit(solution)/shard_map/slice | solution.py:334
  1.2 4.1 %collective-permute-start.17 = (bf16[128,1280]{1,0:T(8,128)(2,1)S(1)}, bf16[128,1280]{1,0:T(8,128)(2,1)S(1)}, u32[]{:S(2)}, u32[]{:S(2)}) collective-permute-start(bf16[128,1280]{1,0:T(8,128)(2,1)S(1)} %get-tuple-element.15), channel_id=1, source_target_pairs={{0,8},{2,10},{4,12},{6,14},{8,0},{10,2},{12,4},{14,6},{1,9},{3,11}... | collective-permute-start | bytes 983048 | tf_op jit(solution)/shard_map/ppermute | solution.py:291
  5.9 1.3 %collective-permute-start.8 = (bf16[128,2560]{1,0:T(8,128)(2,1)}, bf16[128,2560]{1,0:T(8,128)(2,1)S(1)}, u32[]{:S(2)}, u32[]{:S(2)}) collective-permute-start(bf16[128,2560]{1,0:T(8,128)(2,1)} %refs_1_.3), channel_id=1, source_target_pairs={{2,0},{4,6},{10,8},{12,14},{3,1},{5,7},{11,9},{13,15},{18,16},{20,... | collective-permute-start | bytes 1966088 | tf_op jit(solution)/shard_map/ppermute | solution.py:291
  7.2 1.3 %collective-permute-start.1 = (bf16[128,2560]{1,0:T(8,128)(2,1)S(1)}, bf16[128,2560]{1,0:T(8,128)(2,1)}, u32[]{:S(2)}, u32[]{:S(2)}) collective-permute-start(bf16[128,2560]{1,0:T(8,128)(2,1)S(1)} %copy-done.2), channel_id=1, source_target_pairs={{2,0},{4,6},{10,8},{12,14},{3,1},{5,7},{11,9},{13,15},{18,16},{20,... | collective-permute-start | bytes 1966088 | tf_op jit(solution)/shard_map/ppermute | solution.py:291
  8.5 11.6 %collective-permute-done.17.refs_1_ = bf16[128,1280]{1,0:T(8,128)(2,1)S(1)} collective-permute-done((bf16[128,1280]{1,0:T(8,128)(2,1)S(1)}, bf16[128,1280]{1,0:T(8,128)(2,1)S(1)}, u32[]{:S(2)}, u32[]{:S(2)}) %collective-permute-start.17) | collective-permute-done | bytes 327712 | tf_op jit(solution)/shard_map/ppermute | solution.py:291
  20.1 0.7 copy-done.8
  20.8 16.8 %collective-permute-done.15.refs_1_ = bf16[128,1280]{1,0:T(8,128)(2,1)S(1)} collective-permute-done((bf16[128,1280]{1,0:T(8,128)(2,1)S(1)}, bf16[128,1280]{1,0:T(8,128)(2,1)S(1)}, u32[]{:S(2)}, u32[]{:S(2)}) %collective-permute-start.15) | collective-permute-done | bytes 327712 | tf_op jit(solution)/shard_map/ppermute | solution.py:291
  37.6 1.5 %collective-permute-start.2 = (bf16[128,2560]{1,0:T(8,128)(2,1)S(1)}, bf16[128,2560]{1,0:T(8,128)(2,1)}, u32[]{:S(2)}, u32[]{:S(2)}) collective-permute-start(bf16[128,2560]{1,0:T(8,128)(2,1)S(1)} %copy-done.2), channel_id=1, source_target_pairs={{2,4},{4,2},{10,12},{12,10},{3,5},{5,3},{11,13},{13,11},{18,20},{2... | collective-permute-start | bytes 1966088 | tf_op jit(solution)/shard_map/ppermute | solution.py:291
  39.2 1.3 %collective-permute-start.11 = (bf16[128,2560]{1,0:T(8,128)(2,1)S(1)}, bf16[128,2560]{1,0:T(8,128)(2,1)S(1)}, u32[]{:S(2)}, u32[]{:S(2)}) collective-permute-start(bf16[128,2560]{1,0:T(8,128)(2,1)S(1)} %copy-done.1), channel_id=1, source_target_pairs={{2,0},{4,6},{10,8},{12,14},{3,1},{5,7},{11,9},{13,15},{18,16},{20,... | collective-permute-start | bytes 1966088 | tf_op jit(solution)/shard_map/ppermute | solution.py:291
  40.5 0.7 collective-permute-start.12
  41.2 3.3 %shard_map.55 = (bf16[128,2560]{1,0:T(8,128)(2,1)}, f32[128,128]{1,0:T(8,128)S(1)}) custom-call(bf16[128,2560]{1,0:T(8,128)(2,1)S(1)} %collective-permute-done.8.refs_0_, bf16[128,2560]{1,0:T(8,128)(2,1)S(1)} %copy-done.2, bf16[128,2560]{1,0:T(8,128)(2,1)S(1)} %collective-permute-done.refs_2_.refs_3_, bf16[128,2560]{1,0:T(8,128)(2,1)S(1)} %copy-done.1, ...), custom_call_target="tpu_custom_call" | custom-call | flops 335544320 | bytes 3932160 | tf_op jit(solution)/shard_map/pallas_call | solution.py:181
  44.5 9.1 %collective-permute-start.9 = (bf16[128,2560]{1,0:T(8,128)(2,1)}, bf16[128,2560]{1,0:T(8,128)(2,1)}, u32[]{:S(2)}, u32[]{:S(2)}) collective-permute-start(bf16[128,2560]{1,0:T(8,128)(2,1)} %get-tuple-element.10), channel_id=1, source_target_pairs={{0,2},{6,4},{8,10},{14,12},{1,3},{7,5},{9,11},{15,13},{16,18},{22,... | collective-permute-start | bytes 1966088 | tf_op jit(solution)/shard_map/ppermute | solution.py:291
  53.7 1.9 %collective-permute-start.3 = (bf16[128,2560]{1,0:T(8,128)(2,1)}, bf16[128,2560]{1,0:T(8,128)(2,1)}, u32[]{:S(2)}, u32[]{:S(2)}) collective-permute-start(bf16[128,2560]{1,0:T(8,128)(2,1)} %collective-permute-done.1.refs_4_), channel_id=1, source_target_pairs={{0,1},{1,0},{6,7},{7,6},{8,9},{9,8},{14,15},{15,14},{16,17},{17,16... | collective-permute-start | bytes 1966088 | tf_op jit(solution)/shard_map/ppermute | solution.py:296
  56.0 1.5 %collective-permute-start.4 = (bf16[128,2560]{1,0:T(8,128)(2,1)}, bf16[128,2560]{1,0:T(8,128)(2,1)}, u32[]{:S(2)}, u32[]{:S(2)}) collective-permute-start(bf16[128,2560]{1,0:T(8,128)(2,1)} %collective-permute-done.2.refs_5_), channel_id=1, source_target_pairs={{2,3},{3,2},{4,5},{5,4},{10,11},{11,10},{12,13},{13,12},{18,19},{1... | collective-permute-start | bytes 1966088 | tf_op jit(solution)/shard_map/ppermute | solution.py:296
  57.5 0.9 collective-permute-done.11.refs_2_
  58.4 0.8 copy-done.3
  59.3 28.1 %collective-permute-start.10 = (f32[128,128]{1,0:T(8,128)S(1)}, f32[128,128]{1,0:T(8,128)S(1)}, u32[]{:S(2)}, u32[]{:S(2)}) collective-permute-start(f32[128,128]{1,0:T(8,128)S(1)} %get-tuple-element.11), channel_id=1, source_target_pairs={{0,2},{6,4},{8,10},{14,12},{1,3},{7,5},{9,11},{15,13},{16,18},{22,... | collective-permute-start | bytes 196616 | tf_op jit(solution)/shard_map/ppermute | solution.py:291
  87.5 8.2 %collective-permute-done.10.refs_13_ = f32[128,128]{1,0:T(8,128)S(1)} collective-permute-done((f32[128,128]{1,0:T(8,128)S(1)}, f32[128,128]{1,0:T(8,128)S(1)}, u32[]{:S(2)}, u32[]{:S(2)}) %collective-permute-start.10) | collective-permute-done | bytes 65568 | tf_op jit(solution)/shard_map/ppermute | solution.py:291
  95.7 1.9 %collective-permute-start.13 = (bf16[128,2560]{1,0:T(8,128)(2,1)S(1)}, bf16[128,2560]{1,0:T(8,128)(2,1)S(1)}, u32[]{:S(2)}, u32[]{:S(2)}) collective-permute-start(bf16[128,2560]{1,0:T(8,128)(2,1)S(1)} %collective-permute-done.11.refs_2_), channel_id=1, source_target_pairs={{0,1},{1,0},{6,7},{7,6},{8,9},{9,8},{14,15},{15,14},{16,17},{17,16... | collective-permute-start | bytes 1966088 | tf_op jit(solution)/shard_map/ppermute | solution.py:296
  97.6 0.7 collective-permute-start.14
  99.9 1.1 %copy-done.5 = bf16[128,2560]{1,0:T(8,128)(2,1)S(1)} copy-done((bf16[128,2560]{1,0:T(8,128)(2,1)S(1)}, bf16[128,2560]{1,0:T(8,128)(2,1)}, u32[]{:S(2)}) %copy-start.5) | copy-done | bytes 655384
  101.0 6.6 %shard_map.56 = (f32[128,2560]{1,0:T(8,128)S(1)}, bf16[128,5120]{1,0:T(8,128)(2,1)S(1)}, bf16[128,5120]{1,0:T(8,128)(2,1)S(1)}) custom-call(f32[3]{0:T(128)S(1)} %compare_select_fusion.refs_0_, bf16[128,2560]{1,0:T(8,128)(2,1)S(1)} %copy-done.5, bf16[128,2560]{1,0:T(8,128)(2,1)S(1)} %copy-done.2, bf16[128,2560]{1,0:T(8,128)(2,1)S(1)} %collective-permute-done.refs_2_.refs_3_, ...), custom_call_target="tpu_custom_call" | custom-call | flops 1006632960 | bytes 9175040 | tf_op jit(solution)/shard_map/pallas_call | solution.py:181
  108.6 1.0 shard_map.58.refs_3_
  109.7 1.0 shard_map.59
  (44 shorter events, 3.5 us)
Async XLA Ops:
  0.0 98.3 %copy-start = (s32[8,5]{1,0:T(8,128)S(1)}, s32[8,5]{1,0:T(8,128)}, u32[]{:S(2)}) copy-start(s32[8,5]{1,0:T(8,128)} %param.8) | copy-start | bytes 484
  0.0 5.4 %copy-start.1 = (bf16[128,2560]{1,0:T(8,128)(2,1)S(1)}, bf16[128,2560]{1,0:T(8,128)(2,1)}, u32[]{:S(2)}) copy-start(bf16[128,2560]{1,0:T(8,128)(2,1)} %refs_10_.1) | copy-start | bytes 1966084
  0.0 5.4 %copy-start.2 = (bf16[128,2560]{1,0:T(8,128)(2,1)S(1)}, bf16[128,2560]{1,0:T(8,128)(2,1)}, u32[]{:S(2)}) copy-start(bf16[128,2560]{1,0:T(8,128)(2,1)} %refs_2_.1) | copy-start | bytes 1966084
  1.2 18.9 %collective-permute-start.17 = (bf16[128,1280]{1,0:T(8,128)(2,1)S(1)}, bf16[128,1280]{1,0:T(8,128)(2,1)S(1)}, u32[]{:S(2)}, u32[]{:S(2)}) collective-permute-start(bf16[128,1280]{1,0:T(8,128)(2,1)S(1)} %get-tuple-element.15), channel_id=1, source_target_pairs={{0,8},{2,10},{4,12},{6,14},{8,0},{10,2},{12,4},{14,6},{1,9},{3,11}... | collective-permute-start | bytes 983048 | tf_op jit(solution)/shard_map/ppermute | solution.py:291
  5.4 33.8 %collective-permute-start = (bf16[128,2560]{1,0:T(8,128)(2,1)S(1)}, bf16[128,2560]{1,0:T(8,128)(2,1)S(1)}, u32[]{:S(2)}, u32[]{:S(2)}) collective-permute-start(bf16[128,2560]{1,0:T(8,128)(2,1)S(1)} %copy-done.2), channel_id=1, source_target_pairs={{0,1},{1,0},{2,3},{3,2},{4,5},{5,4},{6,7},{7,6},{8,9},{9,8},{10,11... | collective-permute-start | bytes 1966088 | tf_op jit(solution)/shard_map/ppermute | solution.py:296
  5.4 33.8 %collective-permute-start.7 = (bf16[128,2560]{1,0:T(8,128)(2,1)S(1)}, bf16[128,2560]{1,0:T(8,128)(2,1)S(1)}, u32[]{:S(2)}, u32[]{:S(2)}) collective-permute-start(bf16[128,2560]{1,0:T(8,128)(2,1)S(1)} %copy-done.1), channel_id=1, source_target_pairs={{0,1},{1,0},{2,3},{3,2},{4,5},{5,4},{6,7},{7,6},{8,9},{9,8},{10,11... | collective-permute-start | bytes 1966088 | tf_op jit(solution)/shard_map/ppermute | solution.py:296
  5.9 34.6 %collective-permute-start.8 = (bf16[128,2560]{1,0:T(8,128)(2,1)}, bf16[128,2560]{1,0:T(8,128)(2,1)S(1)}, u32[]{:S(2)}, u32[]{:S(2)}) collective-permute-start(bf16[128,2560]{1,0:T(8,128)(2,1)} %refs_1_.3), channel_id=1, source_target_pairs={{2,0},{4,6},{10,8},{12,14},{3,1},{5,7},{11,9},{13,15},{18,16},{20,... | collective-permute-start | bytes 1966088 | tf_op jit(solution)/shard_map/ppermute | solution.py:291
  7.2 37.4 %collective-permute-start.1 = (bf16[128,2560]{1,0:T(8,128)(2,1)S(1)}, bf16[128,2560]{1,0:T(8,128)(2,1)}, u32[]{:S(2)}, u32[]{:S(2)}) collective-permute-start(bf16[128,2560]{1,0:T(8,128)(2,1)S(1)} %copy-done.2), channel_id=1, source_target_pairs={{2,0},{4,6},{10,8},{12,14},{3,1},{5,7},{11,9},{13,15},{18,16},{20,... | collective-permute-start | bytes 1966088 | tf_op jit(solution)/shard_map/ppermute | solution.py:291
  20.8 16.8 %collective-permute-start.15 = (bf16[128,1280]{1,0:T(8,128)(2,1)S(1)}, bf16[128,1280]{1,0:T(8,128)(2,1)S(1)}, u32[]{:S(2)}, u32[]{:S(2)}) collective-permute-start(bf16[128,1280]{1,0:T(8,128)(2,1)S(1)} %get-tuple-element.16), channel_id=1, source_target_pairs={{0,8},{2,10},{4,12},{6,14},{8,0},{10,2},{12,4},{14,6},{1,9},{3,11}... | collective-permute-start | bytes 983048 | tf_op jit(solution)/shard_map/ppermute | solution.py:291
  37.6 1.5 %copy-start.6 = (bf16[128,1280]{1,0:T(8,128)(2,1)}, bf16[128,1280]{1,0:T(8,128)(2,1)S(1)}, u32[]{:S(2)}) copy-start(bf16[128,1280]{1,0:T(8,128)(2,1)S(1)} %collective-permute-done.15.refs_1_) | copy-start | bytes 983044
  37.6 16.0 %collective-permute-start.2 = (bf16[128,2560]{1,0:T(8,128)(2,1)S(1)}, bf16[128,2560]{1,0:T(8,128)(2,1)}, u32[]{:S(2)}, u32[]{:S(2)}) collective-permute-start(bf16[128,2560]{1,0:T(8,128)(2,1)S(1)} %copy-done.2), channel_id=1, source_target_pairs={{2,4},{4,2},{10,12},{12,10},{3,5},{5,3},{11,13},{13,11},{18,20},{2... | collective-permute-start | bytes 1966088 | tf_op jit(solution)/shard_map/ppermute | solution.py:291
  39.2 16.9 %collective-permute-start.5 = (bf16[128,2560]{1,0:T(8,128)(2,1)S(1)}, bf16[128,2560]{1,0:T(8,128)(2,1)}, u32[]{:S(2)}, u32[]{:S(2)}) collective-permute-start(bf16[128,2560]{1,0:T(8,128)(2,1)S(1)} %copy-done.2), channel_id=1, source_target_pairs={{0,8},{2,10},{4,12},{6,14},{8,0},{10,2},{12,4},{14,6},{1,9},{3,11}... | collective-permute-start | bytes 1966088 | tf_op jit(solution)/shard_map/ppermute | solution.py:291
  39.2 19.3 %collective-permute-start.11 = (bf16[128,2560]{1,0:T(8,128)(2,1)S(1)}, bf16[128,2560]{1,0:T(8,128)(2,1)S(1)}, u32[]{:S(2)}, u32[]{:S(2)}) collective-permute-start(bf16[128,2560]{1,0:T(8,128)(2,1)S(1)} %copy-done.1), channel_id=1, source_target_pairs={{2,0},{4,6},{10,8},{12,14},{3,1},{5,7},{11,9},{13,15},{18,16},{20,... | collective-permute-start | bytes 1966088 | tf_op jit(solution)/shard_map/ppermute | solution.py:291
  40.5 18.0 %collective-permute-start.12 = (bf16[128,2560]{1,0:T(8,128)(2,1)S(1)}, bf16[128,2560]{1,0:T(8,128)(2,1)S(1)}, u32[]{:S(2)}, u32[]{:S(2)}) collective-permute-start(bf16[128,2560]{1,0:T(8,128)(2,1)S(1)} %copy-done.1), channel_id=1, source_target_pairs={{2,4},{4,2},{10,12},{12,10},{3,5},{5,3},{11,13},{13,11},{18,20},{2... | collective-permute-start | bytes 1966088 | tf_op jit(solution)/shard_map/ppermute | solution.py:291
  44.5 53.0 %collective-permute-start.9 = (bf16[128,2560]{1,0:T(8,128)(2,1)}, bf16[128,2560]{1,0:T(8,128)(2,1)}, u32[]{:S(2)}, u32[]{:S(2)}) collective-permute-start(bf16[128,2560]{1,0:T(8,128)(2,1)} %get-tuple-element.10), channel_id=1, source_target_pairs={{0,2},{6,4},{8,10},{14,12},{1,3},{7,5},{9,11},{15,13},{16,18},{22,... | collective-permute-start | bytes 1966088 | tf_op jit(solution)/shard_map/ppermute | solution.py:291
  53.7 45.6 %collective-permute-start.3 = (bf16[128,2560]{1,0:T(8,128)(2,1)}, bf16[128,2560]{1,0:T(8,128)(2,1)}, u32[]{:S(2)}, u32[]{:S(2)}) collective-permute-start(bf16[128,2560]{1,0:T(8,128)(2,1)} %collective-permute-done.1.refs_4_), channel_id=1, source_target_pairs={{0,1},{1,0},{6,7},{7,6},{8,9},{9,8},{14,15},{15,14},{16,17},{17,16... | collective-permute-start | bytes 1966088 | tf_op jit(solution)/shard_map/ppermute | solution.py:296
  56.0 43.8 %collective-permute-start.4 = (bf16[128,2560]{1,0:T(8,128)(2,1)}, bf16[128,2560]{1,0:T(8,128)(2,1)}, u32[]{:S(2)}, u32[]{:S(2)}) collective-permute-start(bf16[128,2560]{1,0:T(8,128)(2,1)} %collective-permute-done.2.refs_5_), channel_id=1, source_target_pairs={{2,3},{3,2},{4,5},{5,4},{10,11},{11,10},{12,13},{13,12},{18,19},{1... | collective-permute-start | bytes 1966088 | tf_op jit(solution)/shard_map/ppermute | solution.py:296
  58.4 41.4 %collective-permute-start.6 = (bf16[128,2560]{1,0:T(8,128)(2,1)}, bf16[128,2560]{1,0:T(8,128)(2,1)}, u32[]{:S(2)}, u32[]{:S(2)}) collective-permute-start(bf16[128,2560]{1,0:T(8,128)(2,1)} %collective-permute-done.5.refs_8_), channel_id=1, source_target_pairs={{0,1},{1,0},{2,3},{3,2},{4,5},{5,4},{6,7},{7,6},{8,9},{9,8},{10,11... | collective-permute-start | bytes 1966088 | tf_op jit(solution)/shard_map/ppermute | solution.py:296
  59.3 36.4 %collective-permute-start.10 = (f32[128,128]{1,0:T(8,128)S(1)}, f32[128,128]{1,0:T(8,128)S(1)}, u32[]{:S(2)}, u32[]{:S(2)}) collective-permute-start(f32[128,128]{1,0:T(8,128)S(1)} %get-tuple-element.11), channel_id=1, source_target_pairs={{0,2},{6,4},{8,10},{14,12},{1,3},{7,5},{9,11},{15,13},{16,18},{22,... | collective-permute-start | bytes 196616 | tf_op jit(solution)/shard_map/ppermute | solution.py:291
  95.7 12.0 %collective-permute-start.13 = (bf16[128,2560]{1,0:T(8,128)(2,1)S(1)}, bf16[128,2560]{1,0:T(8,128)(2,1)S(1)}, u32[]{:S(2)}, u32[]{:S(2)}) collective-permute-start(bf16[128,2560]{1,0:T(8,128)(2,1)S(1)} %collective-permute-done.11.refs_2_), channel_id=1, source_target_pairs={{0,1},{1,0},{6,7},{7,6},{8,9},{9,8},{14,15},{15,14},{16,17},{17,16... | collective-permute-start | bytes 1966088 | tf_op jit(solution)/shard_map/ppermute | solution.py:296
  97.6 10.1 %collective-permute-start.14 = (bf16[128,2560]{1,0:T(8,128)(2,1)}, bf16[128,2560]{1,0:T(8,128)(2,1)S(1)}, u32[]{:S(2)}, u32[]{:S(2)}) collective-permute-start(bf16[128,2560]{1,0:T(8,128)(2,1)} %copy-done.3), channel_id=1, source_target_pairs={{2,3},{3,2},{4,5},{5,4},{10,11},{11,10},{12,13},{13,12},{18,19},{1... | collective-permute-start | bytes 1966088 | tf_op jit(solution)/shard_map/ppermute | solution.py:296
  99.2 9.2 %collective-permute-start.18 = (bf16[128,1280]{1,0:T(8,128)(2,1)}, bf16[128,1280]{1,0:T(8,128)(2,1)S(1)}, u32[]{:S(2)}, u32[]{:S(2)}) collective-permute-start(bf16[128,1280]{1,0:T(8,128)(2,1)} %copy-done.8), channel_id=1, source_target_pairs={{0,1},{1,0},{2,3},{3,2},{4,5},{5,4},{6,7},{7,6},{8,9},{9,8},{10,11... | collective-permute-start | bytes 983048 | tf_op jit(solution)/shard_map/ppermute | solution.py:296
  99.8 9.9 %collective-permute-start.16 = (bf16[128,1280]{1,0:T(8,128)(2,1)}, bf16[128,1280]{1,0:T(8,128)(2,1)S(1)}, u32[]{:S(2)}, u32[]{:S(2)}) collective-permute-start(bf16[128,1280]{1,0:T(8,128)(2,1)} %copy-done.6), channel_id=1, source_target_pairs={{0,1},{1,0},{2,3},{3,2},{4,5},{5,4},{6,7},{7,6},{8,9},{9,8},{10,11... | collective-permute-start | bytes 983048 | tf_op jit(solution)/shard_map/ppermute | solution.py:296
  99.9 7.8 %copy-start.4 = (bf16[128,2560]{1,0:T(8,128)(2,1)S(1)}, bf16[128,2560]{1,0:T(8,128)(2,1)}, u32[]{:S(2)}) copy-start(bf16[128,2560]{1,0:T(8,128)(2,1)} %copy-done.3) | copy-start | bytes 1966084
  (5 other events, 4.7 us)
where the time goes:
time: 111 us
  starting transfers between devices  54.7 us (49%)
  waiting for transfers between devices  38 us (34%)
  Pallas kernels  12.7 us (11%)
  local copies, waits for them, and re-layouts  4.92 us (4%)
    ppermute x10, starting transfers between devices, moved(): return lax.ppermute(value, 'row', sorted(sends.items()))  47.5 us
    ppermute x10, waiting for transfers between devices, moved(): return lax.ppermute(value, 'row', sorted(sends.items()))  38 us
    pallas_call x3, Pallas kernels, call(): return list(run(*scalars, *operands))  10.6 us
    ppermute x9, starting transfers between devices, swapped(): return lax.ppermute(value, ('row', 'col'), pairs)  7.19 us
    unnamed x20, local copies, waits for them, and re-layouts  3 us
  transfers between devices with their start and end apart: 19, of which 5 were waited for; matrix products, arithmetic and copies ran while one was open for 1% of the time, Pallas kernels for 11%

commit v1 on v0

--- a/solution.py
+++ b/solution.py
@@ -72,13 +72,11 @@
     return jnp.broadcast_to(found, stats.shape)
 
 
-def attend_chunk(index, heads, k_pairs, visited, bias_ref, refs, score_ref, weight_ref):
+def attend_chunk(index, heads, k_pairs, bias_ref, refs, score_ref, weight_ref):
     q_ref, *refs = refs
     k_refs, refs = grouped(refs, k_pairs)
     v_refs, refs = refs[:2], refs[2:]
-    if visited:
-        visit_ref, stat_ref, *refs = refs
-    out_ref, *held_refs = refs
+    out_ref, *held_refs, stat_ref = refs
     keys_each = 2 * v_refs[0].shape[0]
     each = keys_each // HD
     kept = {}
@@ -93,21 +91,14 @@
             )
             found = found * SCALE
             if n > 0:
-                found = found + bias_ref[n]
+                found = found + bias_ref[n - 1]
             score_ref[head, :, n * keys_each : (n + 1) * keys_each] = found
 
     def weigh(head, here):
         slices = lanes(score_ref[head])
         top = over_row(jnp.max, jnp.maximum, slices)
-        if visited:
-            before = lane_of(stat_ref, index * heads + head) + bias_ref[0]
-            top = jnp.maximum(top, before)
         weights = [jnp.exp2(s - top) for s in slices]
         total = over_row(jnp.sum, jnp.add, weights)
-        factor = None
-        if visited:
-            factor = jnp.exp2(before - top)
-            total = total + factor
         inverse = 1.0 / total
         for at, w in enumerate(weights):
             n = at // each
@@ -116,23 +107,18 @@
             else:
                 start = head * keys_each + at % each * HD
                 held_refs[n - 1][:, start : start + HD] = (w * inverse).astype(jnp.bfloat16)
-        if not visited:
-            at = lax.broadcasted_iota(jnp.int32, top.shape, 1)
-            stats = held_refs[0]
-            kept_stats = stats[...] if head > 0 else jnp.where(index == 0, 0.0, stats[...])
-            stats[...] = jnp.where(at == index * heads + head, top + jnp.log2(total), kept_stats)
-        kept[head] = (inverse, factor)
+        at = lax.broadcasted_iota(jnp.int32, top.shape, 1)
+        stats = stat_ref[...] if head > 0 else jnp.where(index == 0, 0.0, stat_ref[...])
+        stat_ref[...] = jnp.where(at == index * heads + head, top + jnp.log2(total), stats)
+        kept[head] = inverse
 
     def mix(head, here):
-        inverse, factor = kept.pop(head)
         out = jnp.dot(
             weight_ref[head],
             jnp.concatenate([v[:, here] for v in v_refs], axis=0),
             preferred_element_type=jnp.float32,
         )
-        if visited:
-            out = out + factor * visit_ref[:, here].astype(jnp.float32)
-        out_ref[:, here] = (out * inverse).astype(out_ref.dtype)
+        out_ref[:, here] = (out * kept.pop(head)).astype(out_ref.dtype)
 
     steps = [score, weigh, mix]
     for time in range(heads + len(steps) - 1):
@@ -189,51 +175,59 @@
     )
 
 
-def attend(bias, queries, k_pairs, v_own, visit):
+def attend(bias, queries, k_pairs, v_own, dtype):
     tokens, width = queries.shape
-    held, visited = len(k_pairs) - 1, visit is not None
+    held = len(k_pairs) - 1
     keys = 2 * tokens * len(k_pairs)
 
     def chunk(index, heads, scalar_refs, views, scratch_refs):
-        bias_ref = scalar_refs[0] if visited else None
-        attend_chunk(index, heads, k_pairs, visited, bias_ref, views, *scratch_refs)
-
-    full = jax.ShapeDtypeStruct((tokens, width), jnp.float32 if visited else jnp.bfloat16)
+        bias_ref = scalar_refs[0] if held else None
+        attend_chunk(index, heads, k_pairs, bias_ref, views, *scratch_refs)
+
     weight = jax.ShapeDtypeStruct((tokens, 2 * tokens * (width // HD)), jnp.bfloat16)
-    outs = [full] + [weight] * held
-    outs += [] if visited else [jax.ShapeDtypeStruct((tokens, HD), jnp.float32)]
-    operands = [queries] + flat(k_pairs) + flat([v_own]) + (list(visit) if visited else [])
+    outs = [jax.ShapeDtypeStruct((tokens, width), dtype)] + [weight] * held
+    outs += [jax.ShapeDtypeStruct((tokens, HD), jnp.float32)]
+    operands = [queries] + flat(k_pairs) + flat([v_own])
     scratch = [((tokens, keys), jnp.float32), ((tokens, 2 * tokens), jnp.bfloat16)]
-    scalars = [bias] if visited else []
+    scalars = [bias] if held else []
     return call(chunk, HEADS_AT_ONCE, scalars, operands, outs, scratch, 2, keys)
 
 
-def mix(base, weights, v_pair):
+def mix(bias, base, weights, v_pair, stats, visit, visit_stats):
     tokens = base.shape[0]
 
     def chunk(index, heads, scalar_refs, views, scratch_refs):
-        base_ref, weight_ref, *v_refs, out_ref = views
-        pair = grouped(v_refs, [v_pair])[0][0]
+        base_ref, weight_ref, *refs = views
+        (pair,), refs = grouped(refs, [v_pair])
+        stat_ref, visit_ref, visit_stat_ref, out_ref, share_ref = refs
         for head in range(heads):
             here = slice(head * HD, (head + 1) * HD)
-            out_ref[:, here] = base_ref[:, here] + jnp.dot(
+            out = base_ref[:, here] + jnp.dot(
                 weight_ref[:, head * 2 * tokens : (head + 1) * 2 * tokens],
                 gathered(pair, here),
                 preferred_element_type=jnp.float32,
             )
-
-    outs = [jax.ShapeDtypeStruct(base.shape, base.dtype)]
-    operands = [base, weights] + flat([v_pair])
-    return call(chunk, 10, [], operands, outs, [], 1, 2 * tokens)[0]
-
-
-def finish(part, parts, base, weights, v_pairs, dtype, so_far):
+            mine = lane_of(stat_ref, index * heads + head)
+            theirs = lane_of(visit_stat_ref, index * heads + head) + scalar_refs[0][0]
+            top = jnp.maximum(mine, theirs)
+            mine, theirs = jnp.exp2(mine - top), jnp.exp2(theirs - top)
+            inverse = 1.0 / (mine + theirs)
+            share = mine * inverse
+            share_ref[:, here] = share
+            out_ref[:, here] = share * out + (theirs * inverse) * visit_ref[:, here].astype(jnp.float32)
+
+    outs = [jax.ShapeDtypeStruct(base.shape, base.dtype)] * 2
+    operands = [base, weights] + flat([v_pair]) + [stats, visit, visit_stats]
+    return call(chunk, 10, [bias], operands, outs, [], 1, 2 * tokens)
+
+
+def finish(part, parts, base, share, weights, v_pairs, dtype, so_far):
     tokens, width = base.shape
     blocks, heads = len(v_pairs), width // HD // parts
     at_once = divisor(heads, 5)
     started, cols = part * heads * HD, heads * HD
 
-    def kernel(base_ref, *refs):
+    def kernel(base_ref, share_ref, *refs):
         weight_refs, refs = refs[:blocks], refs[blocks:]
         v_refs, refs = refs[: 2 * blocks], refs[2 * blocks :]
         out_ref, held_ref, sems = refs[-3:]
@@ -250,7 +244,7 @@
                     jnp.concatenate(chosen, axis=0),
                     preferred_element_type=jnp.float32,
                 )
-                held_ref[:, here] = (base_ref[:, there] + out).astype(held_ref.dtype)
+                held_ref[:, here] = (base_ref[:, there] + share_ref[:, there] * out).astype(held_ref.dtype)
             wide = at_once * HD
             copies.append(
                 pltpu.make_async_copy(
@@ -264,7 +258,7 @@
             copy.wait()
 
     whole, anywhere = pl.BlockSpec(memory_space=pltpu.VMEM), pl.BlockSpec(memory_space=pl.ANY)
-    operands = [base] + weights + flat(v_pairs)
+    operands = [base, share] + weights + flat(v_pairs)
     aliases = {} if so_far is None else {len(operands): 0}
     return pl.pallas_call(
         kernel,
@@ -321,14 +315,15 @@
     v_near = moved(values, near)
     k_own, v_own = paired(keys, None), paired(values, None)
 
-    result, stats = attend(None, visitors, [k_own], v_own, None)
+    result, stats = attend(None, visitors, [k_own], v_own, queries.dtype)
     visited = (moved(result, back), moved(stats, back))
 
     k_pairs = [k_own, joined(k_near, k_cross)]
     k_pairs += [paired(k, way[0]) for k, way in zip(k_far, far)]
-    bias = biases(visit, side, *[way[1] for way in far])
-    base, of_side, *weights = attend(bias, queries, k_pairs, v_own, visited)
-    base = mix(base, of_side, joined(v_near, v_cross))
+    bias = biases(side, *[way[1] for way in far])
+    base, of_side, *weights, stats = attend(bias, queries, k_pairs, v_own, jnp.float32)
+    v_side = joined(v_near, v_cross)
+    base, share = mix(biases(visit), base, of_side, v_side, stats, *visited)
     out = None
     for part in range(PARTS):
         here = values[:, part * cut : (part + 1) * cut]
@@ -336,7 +331,7 @@
         for way in far:
             v = moved(here, way[0])
             v_pairs.append(paired(v, way[0]))
-        out = finish(part, PARTS, base, weights, v_pairs, queries.dtype, out)
+        out = finish(part, PARTS, base, share, weights, v_pairs, queries.dtype, out)
     return out
 
 

time: 111 us -> 122 us (1.099)
  waiting for transfers between devices: 38 us -> 75.3 us
  starting transfers between devices: 54.7 us -> 22.6 us
  Pallas kernels: 12.7 us -> 14.8 us
  other arithmetic: 0.19 us -> 2.15 us
    ppermute x10, waiting for transfers between devices: 38 us -> 75.3 us  [moved(): return lax.ppermute(value, 'row', sorted(sends.items()))]
    ppermute x10, starting transfers between devices: 47.5 us -> 14.6 us  [moved(): return lax.ppermute(value, 'row', sorted(sends.items()))]
    broadcast_in_dim x0 -> x1, other arithmetic: none -> 1.97 us  [biases(): live = jnp.sum(jnp.where(here, own_row, 0), axis=1)]
    dynamic_slice x0 -> x1, local copies, waits for them, and re-layouts: none -> 1.23 us  [biases(): picks = jnp.asarray(table, jnp.int32)[row]]
    unnamed x20 -> x16, local copies, waits for them, and re-layouts: 3 us -> 2.43 us
  transfers between devices with their start and end apart: 19 -> 19, of which waited for: 5 -> 4; matrix products, arithmetic and copies ran while one was open for 1% -> 3% of each run, Pallas kernels for 11% -> 11%
where the time goes in v1:
time: 122 us; the launch traced here: 121 us
  waiting for transfers between devices  75.3 us (62%)
  starting transfers between devices  22.6 us (19%)
  Pallas kernels  14.8 us (12%)
  local copies, waits for them, and re-layouts  5.58 us (5%)
  other arithmetic  2.15 us (2%)
    ppermute x10, waiting for transfers between devices, moved(): return lax.ppermute(value, 'row', sorted(sends.items()))  75.3 us
    ppermute x10, starting transfers between devices, moved(): return lax.ppermute(value, 'row', sorted(sends.items()))  14.6 us
    pallas_call x3, Pallas kernels, call(): return list(run(*scalars, *operands))  11.8 us
    ppermute x9, starting transfers between devices, swapped(): return lax.ppermute(value, ('row', 'col'), pairs)  7.98 us
    pallas_call x2, Pallas kernels, finish(): pl.pallas_call(kernel, in_specs=[whole] * len(operands) + [anywhere] * le...  2.99 us
  transfers between devices with their start and end apart: 19, of which 4 were waited for; matrix products, arithmetic and copies ran while one was open for 3% of the time, Pallas kernels for 11%

profile of v1, /device:TPU:0, one launch (start us, length us, event | category | flops | bytes accessed | tf_op | source)
XLA Modules:
  0.0 121.2 jit_solution(9095944249071814199)
XLA Ops:
  0.0 1.2 %fusion.4 = (bf16[128,1280]{1,0:T(8,128)(2,1)S(1)}, bf16[128,1280]{1,0:T(8,128)(2,1)S(1)}) fusion(bf16[128,2560]{1,0:T(8,128)(2,1)} %refs_3_.1), kind=kLoop, calls=%fused_computation.10 | loop fusion | bytes 1310720 | tf_op jit(solution)/shard_map/slice | solution.py:329
  1.2 4.1 %collective-permute-start.17 = (bf16[128,1280]{1,0:T(8,128)(2,1)S(1)}, bf16[128,1280]{1,0:T(8,128)(2,1)S(1)}, u32[]{:S(2)}, u32[]{:S(2)}) collective-permute-start(bf16[128,1280]{1,0:T(8,128)(2,1)S(1)} %get-tuple-element.21), channel_id=1, source_target_pairs={{0,8},{2,10},{4,12},{6,14},{8,0},{10,2},{12,4},{14,6},{1,9},{3,11}... | collective-permute-start | bytes 983048 | tf_op jit(solution)/shard_map/ppermute | solution.py:285
  5.4 1.3 %collective-permute-start.1 = (bf16[128,2560]{1,0:T(8,128)(2,1)S(1)}, bf16[128,2560]{1,0:T(8,128)(2,1)}, u32[]{:S(2)}, u32[]{:S(2)}) collective-permute-start(bf16[128,2560]{1,0:T(8,128)(2,1)S(1)} %copy-done.1), channel_id=1, source_target_pairs={{2,0},{4,6},{10,8},{12,14},{3,1},{5,7},{11,9},{13,15},{18,16},{20,... | collective-permute-start | bytes 1966088 | tf_op jit(solution)/shard_map/ppermute | solution.py:285
  6.6 1.5 %collective-permute-start.2 = (bf16[128,2560]{1,0:T(8,128)(2,1)S(1)}, bf16[128,2560]{1,0:T(8,128)(2,1)}, u32[]{:S(2)}, u32[]{:S(2)}) collective-permute-start(bf16[128,2560]{1,0:T(8,128)(2,1)S(1)} %copy-done.1), channel_id=1, source_target_pairs={{2,4},{4,2},{10,12},{12,10},{3,5},{5,3},{11,13},{13,11},{18,20},{2... | collective-permute-start | bytes 1966088 | tf_op jit(solution)/shard_map/ppermute | solution.py:285
  8.2 12.8 %collective-permute-done.17.refs_1_ = bf16[128,1280]{1,0:T(8,128)(2,1)S(1)} collective-permute-done((bf16[128,1280]{1,0:T(8,128)(2,1)S(1)}, bf16[128,1280]{1,0:T(8,128)(2,1)S(1)}, u32[]{:S(2)}, u32[]{:S(2)}) %collective-permute-start.17) | collective-permute-done | bytes 327712 | tf_op jit(solution)/shard_map/ppermute | solution.py:285
  21.8 40.6 %collective-permute-done.15.refs_1_ = bf16[128,1280]{1,0:T(8,128)(2,1)} collective-permute-done((bf16[128,1280]{1,0:T(8,128)(2,1)S(1)}, bf16[128,1280]{1,0:T(8,128)(2,1)}, u32[]{:S(2)}, u32[]{:S(2)}) %collective-permute-start.15) | collective-permute-done | bytes 327712 | tf_op jit(solution)/shard_map/ppermute | solution.py:285
  62.4 1.3 %collective-permute-start.12 = (bf16[128,2560]{1,0:T(8,128)(2,1)}, bf16[128,2560]{1,0:T(8,128)(2,1)S(1)}, u32[]{:S(2)}, u32[]{:S(2)}) collective-permute-start(bf16[128,2560]{1,0:T(8,128)(2,1)} %refs_1_.2), channel_id=1, source_target_pairs={{2,0},{4,6},{10,8},{12,14},{3,1},{5,7},{11,9},{13,15},{18,16},{20,... | collective-permute-start | bytes 1966088 | tf_op jit(solution)/shard_map/ppermute | solution.py:285
  63.7 1.3 %collective-permute-start.8 = (bf16[128,2560]{1,0:T(8,128)(2,1)S(1)}, bf16[128,2560]{1,0:T(8,128)(2,1)S(1)}, u32[]{:S(2)}, u32[]{:S(2)}) collective-permute-start(bf16[128,2560]{1,0:T(8,128)(2,1)S(1)} %copy-done), channel_id=1, source_target_pairs={{2,0},{4,6},{10,8},{12,14},{3,1},{5,7},{11,9},{13,15},{18,16},{20,... | collective-permute-start | bytes 1966088 | tf_op jit(solution)/shard_map/ppermute | solution.py:285
  65.0 1.5 %collective-permute-start.9 = (bf16[128,2560]{1,0:T(8,128)(2,1)S(1)}, bf16[128,2560]{1,0:T(8,128)(2,1)}, u32[]{:S(2)}, u32[]{:S(2)}) collective-permute-start(bf16[128,2560]{1,0:T(8,128)(2,1)S(1)} %copy-done), channel_id=1, source_target_pairs={{2,4},{4,2},{10,12},{12,10},{3,5},{5,3},{11,13},{13,11},{18,20},{2... | collective-permute-start | bytes 1966088 | tf_op jit(solution)/shard_map/ppermute | solution.py:285
  66.5 2.4 %collective-permute-start.3 = (bf16[128,2560]{1,0:T(8,128)(2,1)}, bf16[128,2560]{1,0:T(8,128)(2,1)}, u32[]{:S(2)}, u32[]{:S(2)}) collective-permute-start(bf16[128,2560]{1,0:T(8,128)(2,1)} %collective-permute-done.1.refs_4_), channel_id=1, source_target_pairs={{0,1},{1,0},{6,7},{7,6},{8,9},{9,8},{14,15},{15,14},{16,17},{17,16... | collective-permute-start | bytes 1966088 | tf_op jit(solution)/shard_map/ppermute | solution.py:290
  68.9 1.5 %collective-permute-start.4 = (bf16[128,2560]{1,0:T(8,128)(2,1)}, bf16[128,2560]{1,0:T(8,128)(2,1)}, u32[]{:S(2)}, u32[]{:S(2)}) collective-permute-start(bf16[128,2560]{1,0:T(8,128)(2,1)} %collective-permute-done.2.refs_5_), channel_id=1, source_target_pairs={{2,3},{3,2},{4,5},{5,4},{10,11},{11,10},{12,13},{13,12},{18,19},{1... | collective-permute-start | bytes 1966088 | tf_op jit(solution)/shard_map/ppermute | solution.py:290
  70.4 11.6 %collective-permute-done.12.refs_0_ = bf16[128,2560]{1,0:T(8,128)(2,1)S(1)} collective-permute-done((bf16[128,2560]{1,0:T(8,128)(2,1)}, bf16[128,2560]{1,0:T(8,128)(2,1)S(1)}, u32[]{:S(2)}, u32[]{:S(2)}) %collective-permute-start.12) | collective-permute-done | bytes 655392 | tf_op jit(solution)/shard_map/ppermute | solution.py:285
  82.1 2.5 %shard_map.65 = (bf16[128,2560]{1,0:T(8,128)(2,1)S(1)}, f32[128,128]{1,0:T(8,128)S(1)}) custom-call(bf16[128,2560]{1,0:T(8,128)(2,1)S(1)} %collective-permute-done.12.refs_0_, bf16[128,2560]{1,0:T(8,128)(2,1)S(1)} %copy-done.1, bf16[128,2560]{1,0:T(8,128)(2,1)S(1)} %collective-permute-done.refs_3_.refs_2_, bf16[128,2560]{1,0:T(8,128)(2,1)S(1)} %copy-done, ...), custom_call_target="tpu_custom_call" | custom-call | flops 335544320 | bytes 3932160 | tf_op jit(solution)/shard_map/pallas_call | solution.py:167
  85.5 10.2 %collective-permute-done.8.refs_3_ = bf16[128,2560]{1,0:T(8,128)(2,1)S(1)} collective-permute-done((bf16[128,2560]{1,0:T(8,128)(2,1)S(1)}, bf16[128,2560]{1,0:T(8,128)(2,1)S(1)}, u32[]{:S(2)}, u32[]{:S(2)}) %collective-permute-start.8) | collective-permute-done | bytes 655392 | tf_op jit(solution)/shard_map/ppermute | solution.py:285
  96.5 1.4 %collective-permute-start.14 = (f32[128,128]{1,0:T(8,128)S(1)}, f32[128,128]{1,0:T(8,128)S(1)}, u32[]{:S(2)}, u32[]{:S(2)}) collective-permute-start(f32[128,128]{1,0:T(8,128)S(1)} %get-tuple-element.17), channel_id=1, source_target_pairs={{0,2},{6,4},{8,10},{14,12},{1,3},{7,5},{9,11},{15,13},{16,18},{22,... | collective-permute-start | bytes 196616 | tf_op jit(solution)/shard_map/ppermute | solution.py:285
  98.0 1.2 %constant_dynamic-slice_fusion.2 = s32[1,1]{1,0:T(1,128)} fusion(s32[8,1]{1,0:T(8,128)} %constant.31.clone, s32[]{:T(128)S(6)} %select_n.24), kind=kLoop, calls=%fused_computation.6 | loop fusion | bytes 12 | tf_op jit(solution)/shard_map/dynamic_slice | solution.py:304
  99.2 2.1 %collective-permute-start.13 = (bf16[128,2560]{1,0:T(8,128)(2,1)}, bf16[128,2560]{1,0:T(8,128)(2,1)}, u32[]{:S(2)}, u32[]{:S(2)}) collective-permute-start(bf16[128,2560]{1,0:T(8,128)(2,1)} %copy-done.7), channel_id=1, source_target_pairs={{0,2},{6,4},{8,10},{14,12},{1,3},{7,5},{9,11},{15,13},{16,18},{22,... | collective-permute-start | bytes 1966088 | tf_op jit(solution)/shard_map/ppermute | solution.py:285
  101.3 1.9 %collective-permute-start.10 = (bf16[128,2560]{1,0:T(8,128)(2,1)}, bf16[128,2560]{1,0:T(8,128)(2,1)}, u32[]{:S(2)}, u32[]{:S(2)}) collective-permute-start(bf16[128,2560]{1,0:T(8,128)(2,1)} %copy-done.3), channel_id=1, source_target_pairs={{0,1},{1,0},{6,7},{7,6},{8,9},{9,8},{14,15},{15,14},{16,17},{17,16... | collective-permute-start | bytes 1966088 | tf_op jit(solution)/shard_map/ppermute | solution.py:290
  103.2 1.5 %collective-permute-start.11 = (bf16[128,2560]{1,0:T(8,128)(2,1)}, bf16[128,2560]{1,0:T(8,128)(2,1)}, u32[]{:S(2)}, u32[]{:S(2)}) collective-permute-start(bf16[128,2560]{1,0:T(8,128)(2,1)} %collective-permute-done.9.refs_4_), channel_id=1, source_target_pairs={{2,3},{3,2},{4,5},{5,4},{10,11},{11,10},{12,13},{13,12},{18,19},{1... | collective-permute-start | bytes 1966088 | tf_op jit(solution)/shard_map/ppermute | solution.py:290
  104.7 2.0 %fusion.3 = (s32[5]{0:T(128)S(1)}, s32[]{:T(128)}) fusion(s32[8,5]{1,0:T(8,128)} %param.9, s32[]{:T(128)S(6)} %select_n.24, s32[]{:T(128)} %bitcast), kind=kLoop, calls=%fused_computation.9 | loop fusion | flops 14 | bytes 52 | tf_op jit(solution)/shard_map/jit(_where)/broadcast_in_dim | solution.py:306
  108.8 6.3 %shard_map.64 = (f32[128,2560]{1,0:T(8,128)S(1)}, bf16[128,5120]{1,0:T(8,128)(2,1)S(1)}, bf16[128,5120]{1,0:T(8,128)(2,1)S(1)}, f32[128,128]{1,0:T(8,128)S(1)}) custom-call(f32[2]{0:T(128)S(1)} %compare_select_fusion.refs_0_, bf16[128,2560]{1,0:T(8,128)(2,1)S(1)} %copy-done.2, bf16[128,2560]{1,0:T(8,128)(2,1)S(1)} %copy-done.1, ...), custom_call_target="tpu_custom_call" | custom-call | flops 1006632960 | bytes 9175040 | tf_op jit(solution)/shard_map/pallas_call | solution.py:167
  115.2 3.0 %shard_map.66 = (f32[128,2560]{1,0:T(8,128)S(1)}, f32[128,2560]{1,0:T(8,128)S(1)}) custom-call(f32[1]{0:T(128)} %bitcast.1.refs_0_, f32[128,2560]{1,0:T(8,128)S(1)} %get-tuple-element.13.refs_1_, bf16[128,5120]{1,0:T(8,128)(2,1)S(1)} %get-tuple-element.14.refs_2_, bf16[128,2560]{1,0:T(8,128)(2,1)S(1)} %copy-done.4, ...), custom_call_target="tpu_custom_call" | custom-call | flops 167772160 | bytes 2621440 | tf_op jit(solution)/shard_map/pallas_call | solution.py:167
  118.2 1.0 shard_map.67.refs_3_
  119.3 2.0 %shard_map.68 = bf16[128,2560]{1,0:T(8,128)(2,1)} custom-call(f32[128,2560]{1,0:T(8,128)S(1)} %get-tuple-element.18.base_ref, f32[128,2560]{1,0:T(8,128)S(1)} %get-tuple-element.19.share_ref, bf16[128,5120]{1,0:T(8,128)(2,1)S(1)} %get-tuple-element.20.refs_0_, bf16[128,1280]{1,0:T(8,128)(2,1)} %collective-permute-done.15.refs_1_, ...), custom_call_target="tpu_custom_call", output_to_operand_aliasing={{}: (5, {})} | custom-call | flops 83886080 | bytes 1310720 | tf_op jit(solution)/shard_map/pallas_call | solution.py:263
  (41 shorter events, 4.1 us)
Async XLA Ops:
  0.0 62.4 %copy-start = (bf16[128,2560]{1,0:T(8,128)(2,1)S(1)}, bf16[128,2560]{1,0:T(8,128)(2,1)}, u32[]{:S(2)}) copy-start(bf16[128,2560]{1,0:T(8,128)(2,1)} %refs_3_.1) | copy-start | bytes 1966084
  0.0 5.4 %copy-start.1 = (bf16[128,2560]{1,0:T(8,128)(2,1)S(1)}, bf16[128,2560]{1,0:T(8,128)(2,1)}, u32[]{:S(2)}) copy-start(bf16[128,2560]{1,0:T(8,128)(2,1)} %refs_1_.3) | copy-start | bytes 1966084
  1.2 19.8 %collective-permute-start.17 = (bf16[128,1280]{1,0:T(8,128)(2,1)S(1)}, bf16[128,1280]{1,0:T(8,128)(2,1)S(1)}, u32[]{:S(2)}, u32[]{:S(2)}) collective-permute-start(bf16[128,1280]{1,0:T(8,128)(2,1)S(1)} %get-tuple-element.21), channel_id=1, source_target_pairs={{0,8},{2,10},{4,12},{6,14},{8,0},{10,2},{12,4},{14,6},{1,9},{3,11}... | collective-permute-start | bytes 983048 | tf_op jit(solution)/shard_map/ppermute | solution.py:285
  5.4 57.0 %collective-permute-start.1 = (bf16[128,2560]{1,0:T(8,128)(2,1)S(1)}, bf16[128,2560]{1,0:T(8,128)(2,1)}, u32[]{:S(2)}, u32[]{:S(2)}) collective-permute-start(bf16[128,2560]{1,0:T(8,128)(2,1)S(1)} %copy-done.1), channel_id=1, source_target_pairs={{2,0},{4,6},{10,8},{12,14},{3,1},{5,7},{11,9},{13,15},{18,16},{20,... | collective-permute-start | bytes 1966088 | tf_op jit(solution)/shard_map/ppermute | solution.py:285
  6.6 57.0 %collective-permute-start.2 = (bf16[128,2560]{1,0:T(8,128)(2,1)S(1)}, bf16[128,2560]{1,0:T(8,128)(2,1)}, u32[]{:S(2)}, u32[]{:S(2)}) collective-permute-start(bf16[128,2560]{1,0:T(8,128)(2,1)S(1)} %copy-done.1), channel_id=1, source_target_pairs={{2,4},{4,2},{10,12},{12,10},{3,5},{5,3},{11,13},{13,11},{18,20},{2... | collective-permute-start | bytes 1966088 | tf_op jit(solution)/shard_map/ppermute | solution.py:285
  8.2 56.8 %collective-permute-start.5 = (bf16[128,2560]{1,0:T(8,128)(2,1)S(1)}, bf16[128,2560]{1,0:T(8,128)(2,1)}, u32[]{:S(2)}, u32[]{:S(2)}) collective-permute-start(bf16[128,2560]{1,0:T(8,128)(2,1)S(1)} %copy-done.1), channel_id=1, source_target_pairs={{0,8},{2,10},{4,12},{6,14},{8,0},{10,2},{12,4},{14,6},{1,9},{3,11}... | collective-permute-start | bytes 1966088 | tf_op jit(solution)/shard_map/ppermute | solution.py:285
  8.2 58.3 %collective-permute-start = (bf16[128,2560]{1,0:T(8,128)(2,1)S(1)}, bf16[128,2560]{1,0:T(8,128)(2,1)S(1)}, u32[]{:S(2)}, u32[]{:S(2)}) collective-permute-start(bf16[128,2560]{1,0:T(8,128)(2,1)S(1)} %copy-done.1), channel_id=1, source_target_pairs={{0,1},{1,0},{2,3},{3,2},{4,5},{5,4},{6,7},{7,6},{8,9},{9,8},{10,11... | collective-permute-start | bytes 1966088 | tf_op jit(solution)/shard_map/ppermute | solution.py:290
  21.8 87.1 %copy-start.2 = (bf16[128,2560]{1,0:T(8,128)(2,1)S(1)}, bf16[128,2560]{1,0:T(8,128)(2,1)}, u32[]{:S(2)}) copy-start(bf16[128,2560]{1,0:T(8,128)(2,1)} %refs_1_.2) | copy-start | bytes 1966084
  21.8 40.6 %collective-permute-start.15 = (bf16[128,1280]{1,0:T(8,128)(2,1)S(1)}, bf16[128,1280]{1,0:T(8,128)(2,1)}, u32[]{:S(2)}, u32[]{:S(2)}) collective-permute-start(bf16[128,1280]{1,0:T(8,128)(2,1)S(1)} %get-tuple-element.22), channel_id=1, source_target_pairs={{0,8},{2,10},{4,12},{6,14},{8,0},{10,2},{12,4},{14,6},{1,9},{3,11}... | collective-permute-start | bytes 983048 | tf_op jit(solution)/shard_map/ppermute | solution.py:285
  62.4 6.6 %collective-permute-start.7 = (bf16[128,2560]{1,0:T(8,128)(2,1)S(1)}, bf16[128,2560]{1,0:T(8,128)(2,1)S(1)}, u32[]{:S(2)}, u32[]{:S(2)}) collective-permute-start(bf16[128,2560]{1,0:T(8,128)(2,1)S(1)} %copy-done), channel_id=1, source_target_pairs={{0,1},{1,0},{2,3},{3,2},{4,5},{5,4},{6,7},{7,6},{8,9},{9,8},{10,11... | collective-permute-start | bytes 1966088 | tf_op jit(solution)/shard_map/ppermute | solution.py:290
  62.4 19.7 %collective-permute-start.12 = (bf16[128,2560]{1,0:T(8,128)(2,1)}, bf16[128,2560]{1,0:T(8,128)(2,1)S(1)}, u32[]{:S(2)}, u32[]{:S(2)}) collective-permute-start(bf16[128,2560]{1,0:T(8,128)(2,1)} %refs_1_.2), channel_id=1, source_target_pairs={{2,0},{4,6},{10,8},{12,14},{3,1},{5,7},{11,9},{13,15},{18,16},{20,... | collective-permute-start | bytes 1966088 | tf_op jit(solution)/shard_map/ppermute | solution.py:285
  63.7 32.0 %collective-permute-start.8 = (bf16[128,2560]{1,0:T(8,128)(2,1)S(1)}, bf16[128,2560]{1,0:T(8,128)(2,1)S(1)}, u32[]{:S(2)}, u32[]{:S(2)}) collective-permute-start(bf16[128,2560]{1,0:T(8,128)(2,1)S(1)} %copy-done), channel_id=1, source_target_pairs={{2,0},{4,6},{10,8},{12,14},{3,1},{5,7},{11,9},{13,15},{18,16},{20,... | collective-permute-start | bytes 1966088 | tf_op jit(solution)/shard_map/ppermute | solution.py:285
  65.0 34.2 %collective-permute-start.9 = (bf16[128,2560]{1,0:T(8,128)(2,1)S(1)}, bf16[128,2560]{1,0:T(8,128)(2,1)}, u32[]{:S(2)}, u32[]{:S(2)}) collective-permute-start(bf16[128,2560]{1,0:T(8,128)(2,1)S(1)} %copy-done), channel_id=1, source_target_pairs={{2,4},{4,2},{10,12},{12,10},{3,5},{5,3},{11,13},{13,11},{18,20},{2... | collective-permute-start | bytes 1966088 | tf_op jit(solution)/shard_map/ppermute | solution.py:285
  66.5 36.7 %collective-permute-start.3 = (bf16[128,2560]{1,0:T(8,128)(2,1)}, bf16[128,2560]{1,0:T(8,128)(2,1)}, u32[]{:S(2)}, u32[]{:S(2)}) collective-permute-start(bf16[128,2560]{1,0:T(8,128)(2,1)} %collective-permute-done.1.refs_4_), channel_id=1, source_target_pairs={{0,1},{1,0},{6,7},{7,6},{8,9},{9,8},{14,15},{15,14},{16,17},{17,16... | collective-permute-start | bytes 1966088 | tf_op jit(solution)/shard_map/ppermute | solution.py:290
  68.9 39.2 %collective-permute-start.4 = (bf16[128,2560]{1,0:T(8,128)(2,1)}, bf16[128,2560]{1,0:T(8,128)(2,1)}, u32[]{:S(2)}, u32[]{:S(2)}) collective-permute-start(bf16[128,2560]{1,0:T(8,128)(2,1)} %collective-permute-done.2.refs_5_), channel_id=1, source_target_pairs={{2,3},{3,2},{4,5},{5,4},{10,11},{11,10},{12,13},{13,12},{18,19},{1... | collective-permute-start | bytes 1966088 | tf_op jit(solution)/shard_map/ppermute | solution.py:290
  82.1 26.6 %collective-permute-start.6 = (bf16[128,2560]{1,0:T(8,128)(2,1)}, bf16[128,2560]{1,0:T(8,128)(2,1)}, u32[]{:S(2)}, u32[]{:S(2)}) collective-permute-start(bf16[128,2560]{1,0:T(8,128)(2,1)} %collective-permute-done.5.refs_8_), channel_id=1, source_target_pairs={{0,1},{1,0},{2,3},{3,2},{4,5},{5,4},{6,7},{7,6},{8,9},{9,8},{10,11... | collective-permute-start | bytes 1966088 | tf_op jit(solution)/shard_map/ppermute | solution.py:290
  96.5 4.8 %collective-permute-start.14 = (f32[128,128]{1,0:T(8,128)S(1)}, f32[128,128]{1,0:T(8,128)S(1)}, u32[]{:S(2)}, u32[]{:S(2)}) collective-permute-start(f32[128,128]{1,0:T(8,128)S(1)} %get-tuple-element.17), channel_id=1, source_target_pairs={{0,2},{6,4},{8,10},{14,12},{1,3},{7,5},{9,11},{15,13},{16,18},{22,... | collective-permute-start | bytes 196616 | tf_op jit(solution)/shard_map/ppermute | solution.py:285
  99.2 15.9 %collective-permute-start.13 = (bf16[128,2560]{1,0:T(8,128)(2,1)}, bf16[128,2560]{1,0:T(8,128)(2,1)}, u32[]{:S(2)}, u32[]{:S(2)}) collective-permute-start(bf16[128,2560]{1,0:T(8,128)(2,1)} %copy-done.7), channel_id=1, source_target_pairs={{0,2},{6,4},{8,10},{14,12},{1,3},{7,5},{9,11},{15,13},{16,18},{22,... | collective-permute-start | bytes 1966088 | tf_op jit(solution)/shard_map/ppermute | solution.py:285
  101.3 13.8 %collective-permute-start.10 = (bf16[128,2560]{1,0:T(8,128)(2,1)}, bf16[128,2560]{1,0:T(8,128)(2,1)}, u32[]{:S(2)}, u32[]{:S(2)}) collective-permute-start(bf16[128,2560]{1,0:T(8,128)(2,1)} %copy-done.3), channel_id=1, source_target_pairs={{0,1},{1,0},{6,7},{7,6},{8,9},{9,8},{14,15},{15,14},{16,17},{17,16... | collective-permute-start | bytes 1966088 | tf_op jit(solution)/shard_map/ppermute | solution.py:290
  103.2 11.9 %collective-permute-start.11 = (bf16[128,2560]{1,0:T(8,128)(2,1)}, bf16[128,2560]{1,0:T(8,128)(2,1)}, u32[]{:S(2)}, u32[]{:S(2)}) collective-permute-start(bf16[128,2560]{1,0:T(8,128)(2,1)} %collective-permute-done.9.refs_4_), channel_id=1, source_target_pairs={{2,3},{3,2},{4,5},{5,4},{10,11},{11,10},{12,13},{13,12},{18,19},{1... | collective-permute-start | bytes 1966088 | tf_op jit(solution)/shard_map/ppermute | solution.py:290
  108.2 10.0 %collective-permute-start.18 = (bf16[128,1280]{1,0:T(8,128)(2,1)}, bf16[128,1280]{1,0:T(8,128)(2,1)S(1)}, u32[]{:S(2)}, u32[]{:S(2)}) collective-permute-start(bf16[128,1280]{1,0:T(8,128)(2,1)} %copy-done.5), channel_id=1, source_target_pairs={{0,1},{1,0},{2,3},{3,2},{4,5},{5,4},{6,7},{7,6},{8,9},{9,8},{10,11... | collective-permute-start | bytes 983048 | tf_op jit(solution)/shard_map/ppermute | solution.py:290
  108.7 10.5 %collective-permute-start.16 = (bf16[128,1280]{1,0:T(8,128)(2,1)}, bf16[128,1280]{1,0:T(8,128)(2,1)S(1)}, u32[]{:S(2)}, u32[]{:S(2)}) collective-permute-start(bf16[128,1280]{1,0:T(8,128)(2,1)} %collective-permute-done.15.refs_1_), channel_id=1, source_target_pairs={{0,1},{1,0},{2,3},{3,2},{4,5},{5,4},{6,7},{7,6},{8,9},{9,8},{10,11... | collective-permute-start | bytes 983048 | tf_op jit(solution)/shard_map/ppermute | solution.py:290
  108.8 6.3 %copy-start.4 = (bf16[128,2560]{1,0:T(8,128)(2,1)S(1)}, bf16[128,2560]{1,0:T(8,128)(2,1)}, u32[]{:S(2)}) copy-start(bf16[128,2560]{1,0:T(8,128)(2,1)} %copy-done.3) | copy-start | bytes 1966084
  115.2 3.0 %copy-start.6 = (bf16[128,1280]{1,0:T(8,128)(2,1)S(1)}, bf16[128,1280]{1,0:T(8,128)(2,1)}, u32[]{:S(2)}) copy-start(bf16[128,1280]{1,0:T(8,128)(2,1)} %copy-done.5) | copy-start | bytes 983044
  (3 other events, 2.4 us)
